TPU v7x, 128 devices: a whole 4x4x4 slice. The times are simulated.
128 devices in a mesh: ctx: 16 (over x, y_lo, core), ch: 8 (over y_hi, z).
Axes of the slice: x: 4, y: 4 (y_hi: 2, y_lo: 2; y = y_hi * 2 + y_lo), z: 4, core: 2. Of those that a mesh axis runs over, the one named last changes fastest.
Arguments:
- query_in: bfloat16 [3072, 8192], P('ctx', 'ch'), may hold values from -6 to 6
- key_in: bfloat16 [3072, 8192], P('ctx', 'ch'), may hold values from -6 to 6
- value_in: bfloat16 [3072, 8192], P('ctx', 'ch'), may hold values from -6 to 6
- filters: bfloat16 [512, 3072], P('ch'), may hold values from -0.8 to 0.8
- skip_gain: float32 [8192], P('ch'), may hold values from -3 to 3
- out_weight: bfloat16 [8192, 8192], P(None, 'ch'), may hold values from -0.0625 to 0.0625
Outputs:
- output: bfloat16 [3072, 8192], P('ctx', 'ch')
All inputs are finite; a program needn't handle non-finite values.
Results may differ from a plain program's by a relative error of at most 0.0057.
Values may be sent and summed in bfloat16 or wider, within the bound.
No kernel may reach another device: no remote copies, remote signals or barrier semaphores. Data moves between devices by JAX's collectives and lax.ppermute only.
A program may use at most 128 MiB of HBM per device.

v0:
```python
import jax
import jax.numpy as jnp
from jax import lax
from jax.sharding import PartitionSpec as P


def toeplitz(padded, offset, out_rows, src_rows):
    groups = padded.shape[0]
    seq_len = padded.shape[1] // 2
    width = out_rows + src_rows - 1
    segment = lax.dynamic_slice_in_dim(padded, offset - src_rows + 1 + seq_len, width, 1)
    flipped = jnp.concatenate([segment[:, ::-1], jnp.zeros((groups, 1), segment.dtype)], axis=1)
    period = width + 1
    repeated = jnp.broadcast_to(flipped[:, None, :], (groups, out_rows, period)).reshape(
        groups, out_rows * period
    )
    sheared = repeated[:, out_rows - 1 : out_rows - 1 + out_rows * width].reshape(
        groups, out_rows, width
    )
    return sheared[:, :, :src_rows]


def conv_term(padded, offset, out_rows, source):
    tiles = toeplitz(padded, offset, out_rows, source.shape[0])
    grouped = source.reshape(source.shape[0], padded.shape[0], -1)
    result = jnp.einsum("grs,sgc->rgc", tiles, grouped, preferred_element_type=jnp.float32)
    return result.reshape(out_rows, -1)


def causal_add(summed, padded, out_start, out_rows, source, src_start):

    def include(current):
        return current + conv_term(padded, out_start - src_start, out_rows, source)

    def leave(current):
        return current

    return lax.cond(src_start < out_start + out_rows, include, leave, summed)


def apply_gate(query_part, conv, gain, mixed_part):
    total = conv + gain[None, :] * mixed_part.astype(jnp.float32)
    return (query_part.astype(jnp.float32) * total).astype(jnp.bfloat16)


def project(gated, out_weight):
    total = jnp.dot(
        lax.all_gather(gated, "ch", axis=1, tiled=True),
        out_weight,
        preferred_element_type=jnp.float32,
    )
    return total.astype(jnp.bfloat16)


def shards(query_in, key_in, value_in, filters, skip_gain, out_weight):
    block_rows = query_in.shape[0]
    channels = query_in.shape[1]
    cycle_pos = lax.axis_index("ctx")
    mixed = (key_in.astype(jnp.float32) * value_in.astype(jnp.float32)).astype(jnp.bfloat16)
    padded = jnp.concatenate([jnp.zeros_like(filters), filters], axis=1)
    out_start = cycle_pos * block_rows
    empty = jnp.zeros((block_rows, channels), jnp.float32)
    portion = lax.all_gather(mixed, "ctx", axis=0, tiled=True)
    height = portion.shape[0]
    pieces = portion.reshape(height // block_rows, block_rows, channels)

    def advance(running, element):
        position, piece = element
        return (
            causal_add(running, padded, out_start, block_rows, piece, position * block_rows),
            None,
        )

    running, _ = lax.scan(
        advance, empty, (jnp.arange(height // block_rows, dtype=jnp.int32), pieces)
    )
    return project(apply_gate(query_in, running, skip_gain, mixed), out_weight)


def solution(mesh):
    placed = (P("ctx", "ch"), P("ctx", "ch"), P("ctx", "ch"), P("ch", None), P("ch"), P(None, "ch"))
    return jax.shard_map(
        shards, mesh=mesh, in_specs=placed, out_specs=P("ctx", "ch"), check_vma=False
    )
```

profile of v0, /device:TPU:0, one launch (start us, length us, event | category | flops | bytes accessed | tf_op | source)
XLA Modules:
  0.0 1123.3 jit_solution(5549705480522828979)
XLA Ops:
  6.5 0.0 all-gather.3.cloned.1.call-start
  6.5 2.0 multiply_convert_fusion.1
  8.5 0.0 all-gather.3.cloned.1.call-update
  8.6 0.0 all-gather.5.cloned.1.call-start
  8.6 1.1 concatenate.6
  9.7 44.2 %all-gather.3.cloned.1.call-done = bf16[3072,1024]{1,0:T(8,128)(2,1)} async-done(((bf16[192,1024]{1,0:T(8,128)(2,1)}), bf16[3072,1024]{1,0:T(8,128)(2,1)}) %all-gather.3.cloned.1.call-update) | async-done | bytes 6291472 | tf_op jit(solution)/shard_map/all_gather | solution.py:63
  53.9 11.0 copy.11
  64.9 0.1 broadcast_in_dim.5
  65.0 0.0 copy-start
  65.0 0.0 copy-start.1
  65.0 0.0 copy-start.2
  65.0 81.9 %while.14 = (s32[]{:T(128)}, f32[192,1024]{0,1:T(8,128)S(1)}, s32[16]{0:T(128)S(1)}, s32[]{:T(128)}, s32[]{:T(128)}, /*index=5*/bf16[64,6144]{1,0:T(8,128)(2,1)S...) while((s32[]{:T(128)}, f32[192,1024]{0,1:T(8,128)S(1)}, s32[16]{0:T(128)S(1)}, s32[]{:T(128)}, ...), condition=%wide.region_3.4_spmd, body=%wide.region_0.3_spmd.sunk | while | flops 75694096 | bytes 77020792 | solution.py:74
  65.0 0.7 dynamic_slice.19
  66.4 59.7 %conditional.2 = (f32[192,1024]{0,1:T(8,128)S(1)}) conditional(s32[]{:T(128)} %convert_element_type.40, f32[192,1024]{0,1:T(8,128)S(1)} %get-tuple-element.186, (s32[]{:T(128)}, s32[]{:T(128)}, bf16[64,6144]{1,0:T(8,128)(2,1)S(1)}, bf16[16,192,1024]{1,2,0:T(8,128)(2,1)}, s32[]{:T(128)}, /*index=5*/f32[192,1024]{0,1:T(8,128)S(1)}) %tuple.35), branch_computations={%region_1.1_spmd, %region_2.2_spmd} | conditional | flops 75694088 | bytes 77020616 | solution.py:38
  66.4 0.1 constant_dynamic-slice_fusion.1
  66.5 0.3 reverse
  66.7 0.1 slice.12
  66.9 4.5 broadcast_in_dim.1
  71.3 13.3 %copy.13 = bf16[8,8,192,384]{3,1,2,0:T(8,128)(2,1)} copy(bf16[8,8,192,384]{3,2,1,0:T(8,128)(2,1)} %bitcast.15) | data formatting | bytes 18874368 | tf_op jit(solution)/shard_map/while/body/eval_jaxpr/cond
  84.7 9.8 slice.8
  94.5 25.7 %reshape.21 = bf16[64,192,383]{2,1,0:T(8,128)(2,1)} reshape(bf16[64,73536]{1,0:T(8,128)(2,1)} %slice.8) | data formatting | bytes 18825216 | tf_op jit(solution)/shard_map/while/body/eval_jaxpr/cond/branch_1_fun/reshape | solution.py:17
  120.2 1.1 constant_dynamic-slice_fusion
  121.3 4.5 fusion
  125.8 0.2 bitcast_add_fusion
  126.1 0.7 dynamic_slice.19
  127.4 0.7 dynamic_slice.19
  128.8 0.7 dynamic_slice.19
  130.2 0.7 dynamic_slice.19
  131.6 0.7 dynamic_slice.19
  132.9 0.7 dynamic_slice.19
  134.3 0.7 dynamic_slice.19
  135.7 0.7 dynamic_slice.19
  137.1 0.7 dynamic_slice.19
  138.4 0.7 dynamic_slice.19
  139.8 0.7 dynamic_slice.19
  141.2 0.7 dynamic_slice.19
  142.6 0.7 dynamic_slice.19
  143.9 0.7 dynamic_slice.19
  145.3 0.7 dynamic_slice.19
  146.9 0.3 copy.12
  147.2 0.0 copy-done
  147.2 0.0 copy-done.1
  147.2 0.0 copy-done.2
  147.2 0.9 multiply_convert_fusion
  148.1 0.0 all-gather.5.cloned.1.call-update
  148.2 957.4 %all-gather.5.cloned.1.call-done = bf16[192,8192]{1,0:T(8,128)(2,1)} async-done(((bf16[192,1024]{1,0:T(8,128)(2,1)}), bf16[192,8192]{1,0:T(8,128)(2,1)}) %all-gather.5.cloned.1.call-update) | async-done | bytes 3145744 | tf_op jit(solution)/shard_map/all_gather | solution.py:48
  1105.6 10.9 convolution_convert_fusion
  (17 shorter events, 0.2 us)
Async XLA Ops:
  6.5 47.3 %all-gather.3.cloned.1.call-start = ((), (), s32[]{:S(2)}) async-start(), calls=%async_computation | async-start | bytes 6684672 | tf_op jit(solution)/shard_map/all_gather | solution.py:63
  8.6 1097.0 %all-gather.5.cloned.1.call-start = ((), (), s32[]{:S(2)}) async-start(), calls=%async_computation.1 | async-start | bytes 3538944 | tf_op jit(solution)/shard_map/all_gather | solution.py:48
  65.0 82.2 %copy-start = (bf16[192,1024]{1,0:T(8,128)(2,1)S(1)}, bf16[192,1024]{1,0:T(8,128)(2,1)}, u32[]{:S(2)}) copy-start(bf16[192,1024]{1,0:T(8,128)(2,1)} %multiply_convert_fusion.1) | copy-start | bytes 1179652
  65.0 82.2 %copy-start.1 = (bf16[192,1024]{1,0:T(8,128)(2,1)S(1)}, bf16[192,1024]{1,0:T(8,128)(2,1)}, u32[]{:S(2)}) copy-start(bf16[192,1024]{1,0:T(8,128)(2,1)} %param.10) | copy-start | bytes 1179652
  65.0 82.2 %copy-start.2 = (f32[1024]{0:T(1024)S(1)}, f32[1024]{0:T(1024)}, u32[]{:S(2)}) copy-start(f32[1024]{0:T(1024)} %param.14) | copy-start | bytes 12292
Sparse Core Ops, SparseCore 0:
  9.0 44.7 all-gather.2
  148.3 957.2 all-gather.4
where the time goes:
time: 1130 us; the launch traced here: 1120 us
  waiting for transfers between devices  1000 us (88%)
  local copies, waits for them, and re-layouts  77.8 us (7%)
  matrix products  15.4 us (1%)
  between operations  13.5 us (1%)
  loops' own time  11.8 us (1%)
    all_gather x1, waiting for transfers between devices, project(): lax.all_gather(gated, 'ch', axis=1, tiled=True)  957 us
    all_gather x1, waiting for transfers between devices, shards(): portion = lax.all_gather(mixed, 'ctx', axis=0, tiled=True)  44.2 us
    reshape x1, local copies, waits for them, and re-layouts, toeplitz(): repeated[:, out_rows - 1:out_rows - 1 + out_rows * width]  25.7 us
  transfers between devices with their start and end apart: 2, of which 2 were waited for; matrix products, arithmetic and copies ran while one was open for 0% of the time, Pallas kernels for 0%

commit v1 on v0

--- a/solution.py
+++ b/solution.py
@@ -45,7 +45,9 @@
 
 def project(gated, out_weight):
     total = jnp.dot(
-        lax.all_gather(gated, "ch", axis=1, tiled=True),
+        jnp.concatenate(
+            lax.all_to_all(jnp.stack([gated] * lax.axis_size("ch")), "ch", 0, 0), axis=1
+        ),
         out_weight,
         preferred_element_type=jnp.float32,
     )

time: 1130 us -> 1080 us (0.956)
  the two profiles are of different devices: /device:TPU:0 before, /device:TPU:15 now
where the time goes in v1:
time: 1080 us
  local copies, waits for them, and re-layouts  901 us (83%)
  matrix products  76.3 us (7%)
  waiting for transfers between devices  43.5 us (4%)
  blocking collectives  28.8 us (3%)
  between operations  13.5 us (1%)
  loops' own time  11.4 us (1%)
    reshape x16, local copies, waits for them, and re-layouts, toeplitz(): repeated[:, out_rows - 1:out_rows - 1 + out_rows * width]  412 us
    cond x48, local copies, waits for them, and re-layouts  219 us
    slice x16, local copies, waits for them, and re-layouts, toeplitz(): repeated[:, out_rows - 1:out_rows - 1 + out_rows * width]  157 us
    dot_general x16, matrix products, conv_term(): jnp.einsum('grs,sgc->rgc', tiles, grouped, preferred_element_type=jnp.flo...  72 us
    broadcast_in_dim x16, local copies, waits for them, and re-layouts, toeplitz(): jnp.broadcast_to(flipped[:, None, :], (groups, out_rows, period))  71.6 us
    all_gather x1, waiting for transfers between devices, shards(): portion = lax.all_gather(mixed, 'ctx', axis=0, tiled=True)  43.5 us
    all_to_all x1, blocking collectives, project(): lax.all_to_all(jnp.stack([gated] * lax.axis_size('ch')), 'ch', 0, 0)  28.8 us
    dynamic_slice x32, local copies, waits for them, and re-layouts, shards(): lax.scan(advance, empty, (jnp.arange(height // block_rows, dtype=jnp.int3...  26.7 us
  transfers between devices with their start and end apart: 1, of which 1 were waited for; matrix products, arithmetic and copies ran while one was open for 0% of the time, Pallas kernels for 0%

profile of v1, /device:TPU:15, one launch (start us, length us, event | category | flops | bytes accessed | tf_op | source)
XLA Modules:
  0.0 1080.6 jit_solution(12584799485360475080)
XLA Ops:
  9.6 43.5 %all-gather.2.cloned.1.call-done = bf16[3072,1024]{1,0:T(8,128)(2,1)} async-done(((bf16[192,1024]{1,0:T(8,128)(2,1)}), bf16[3072,1024]{1,0:T(8,128)(2,1)}) %all-gather.2.cloned.1.call-update) | async-done | bytes 6291472 | tf_op jit(solution)/shard_map/all_gather | solution.py:65
  64.3 975.0 %while.14 = (s32[]{:T(128)}, f32[192,1024]{0,1:T(8,128)S(1)}, s32[16]{0:T(128)S(1)}, s32[]{:T(128)}, s32[]{:T(128)}, /*index=5*/bf16[64,6144]{1,0:T(8,128)(2,1)S...) while((s32[]{:T(128)}, f32[192,1024]{0,1:T(8,128)S(1)}, s32[16]{0:T(128)S(1)}, s32[]{:T(128)}, ...), condition=%wide.region_3.4_spmd, body=%wide.region_0.3_spmd.sunk | while | flops 75694096 | bytes 77020792 | solution.py:76
  65.5 59.7 %conditional.2 = (f32[192,1024]{0,1:T(8,128)S(1)}) conditional(s32[]{:T(128)} %convert_element_type.40, f32[192,1024]{0,1:T(8,128)S(1)} %get-tuple-element.193, (s32[]{:T(128)}, s32[]{:T(128)}, bf16[64,6144]{1,0:T(8,128)(2,1)S(1)}, bf16[16,192,1024]{1,2,0:T(8,128)(2,1)}, s32[]{:T(128)}, /*index=5*/f32[192,1024]{0,1:T(8,128)S(1)}) %tuple.36), branch_computations={%region_1.1_spmd, %region_2.2_spmd} | conditional | flops 75694088 | bytes 77020616 | solution.py:38
  70.5 13.3 %copy.17 = bf16[8,8,192,384]{3,1,2,0:T(8,128)(2,1)} copy(bf16[8,8,192,384]{3,2,1,0:T(8,128)(2,1)} %bitcast.18) | data formatting | bytes 18874368 | tf_op jit(solution)/shard_map/while/body/eval_jaxpr/cond
  93.7 25.7 %reshape.27 = bf16[64,192,383]{2,1,0:T(8,128)(2,1)} reshape(bf16[64,73536]{1,0:T(8,128)(2,1)} %slice.8) | data formatting | bytes 18825216 | tf_op jit(solution)/shard_map/while/body/eval_jaxpr/cond/branch_1_fun/reshape | solution.py:17
  126.4 59.7 %conditional.2 = (f32[192,1024]{0,1:T(8,128)S(1)}) conditional(s32[]{:T(128)} %convert_element_type.40, f32[192,1024]{0,1:T(8,128)S(1)} %get-tuple-element.193, (s32[]{:T(128)}, s32[]{:T(128)}, bf16[64,6144]{1,0:T(8,128)(2,1)S(1)}, bf16[16,192,1024]{1,2,0:T(8,128)(2,1)}, s32[]{:T(128)}, /*index=5*/f32[192,1024]{0,1:T(8,128)S(1)}) %tuple.36), branch_computations={%region_1.1_spmd, %region_2.2_spmd} | conditional | flops 75694088 | bytes 77020616 | solution.py:38
  131.4 13.3 %copy.17 = bf16[8,8,192,384]{3,1,2,0:T(8,128)(2,1)} copy(bf16[8,8,192,384]{3,2,1,0:T(8,128)(2,1)} %bitcast.18) | data formatting | bytes 18874368 | tf_op jit(solution)/shard_map/while/body/eval_jaxpr/cond
  154.6 25.7 %reshape.27 = bf16[64,192,383]{2,1,0:T(8,128)(2,1)} reshape(bf16[64,73536]{1,0:T(8,128)(2,1)} %slice.8) | data formatting | bytes 18825216 | tf_op jit(solution)/shard_map/while/body/eval_jaxpr/cond/branch_1_fun/reshape | solution.py:17
  187.4 59.7 %conditional.2 = (f32[192,1024]{0,1:T(8,128)S(1)}) conditional(s32[]{:T(128)} %convert_element_type.40, f32[192,1024]{0,1:T(8,128)S(1)} %get-tuple-element.193, (s32[]{:T(128)}, s32[]{:T(128)}, bf16[64,6144]{1,0:T(8,128)(2,1)S(1)}, bf16[16,192,1024]{1,2,0:T(8,128)(2,1)}, s32[]{:T(128)}, /*index=5*/f32[192,1024]{0,1:T(8,128)S(1)}) %tuple.36), branch_computations={%region_1.1_spmd, %region_2.2_spmd} | conditional | flops 75694088 | bytes 77020616 | solution.py:38
  192.4 13.3 %copy.17 = bf16[8,8,192,384]{3,1,2,0:T(8,128)(2,1)} copy(bf16[8,8,192,384]{3,2,1,0:T(8,128)(2,1)} %bitcast.18) | data formatting | bytes 18874368 | tf_op jit(solution)/shard_map/while/body/eval_jaxpr/cond
  215.5 25.7 %reshape.27 = bf16[64,192,383]{2,1,0:T(8,128)(2,1)} reshape(bf16[64,73536]{1,0:T(8,128)(2,1)} %slice.8) | data formatting | bytes 18825216 | tf_op jit(solution)/shard_map/while/body/eval_jaxpr/cond/branch_1_fun/reshape | solution.py:17
  248.3 59.7 %conditional.2 = (f32[192,1024]{0,1:T(8,128)S(1)}) conditional(s32[]{:T(128)} %convert_element_type.40, f32[192,1024]{0,1:T(8,128)S(1)} %get-tuple-element.193, (s32[]{:T(128)}, s32[]{:T(128)}, bf16[64,6144]{1,0:T(8,128)(2,1)S(1)}, bf16[16,192,1024]{1,2,0:T(8,128)(2,1)}, s32[]{:T(128)}, /*index=5*/f32[192,1024]{0,1:T(8,128)S(1)}) %tuple.36), branch_computations={%region_1.1_spmd, %region_2.2_spmd} | conditional | flops 75694088 | bytes 77020616 | solution.py:38
  253.3 13.3 %copy.17 = bf16[8,8,192,384]{3,1,2,0:T(8,128)(2,1)} copy(bf16[8,8,192,384]{3,2,1,0:T(8,128)(2,1)} %bitcast.18) | data formatting | bytes 18874368 | tf_op jit(solution)/shard_map/while/body/eval_jaxpr/cond
  276.4 25.7 %reshape.27 = bf16[64,192,383]{2,1,0:T(8,128)(2,1)} reshape(bf16[64,73536]{1,0:T(8,128)(2,1)} %slice.8) | data formatting | bytes 18825216 | tf_op jit(solution)/shard_map/while/body/eval_jaxpr/cond/branch_1_fun/reshape | solution.py:17
  309.2 59.7 %conditional.2 = (f32[192,1024]{0,1:T(8,128)S(1)}) conditional(s32[]{:T(128)} %convert_element_type.40, f32[192,1024]{0,1:T(8,128)S(1)} %get-tuple-element.193, (s32[]{:T(128)}, s32[]{:T(128)}, bf16[64,6144]{1,0:T(8,128)(2,1)S(1)}, bf16[16,192,1024]{1,2,0:T(8,128)(2,1)}, s32[]{:T(128)}, /*index=5*/f32[192,1024]{0,1:T(8,128)S(1)}) %tuple.36), branch_computations={%region_1.1_spmd, %region_2.2_spmd} | conditional | flops 75694088 | bytes 77020616 | solution.py:38
  314.2 13.3 %copy.17 = bf16[8,8,192,384]{3,1,2,0:T(8,128)(2,1)} copy(bf16[8,8,192,384]{3,2,1,0:T(8,128)(2,1)} %bitcast.18) | data formatting | bytes 18874368 | tf_op jit(solution)/shard_map/while/body/eval_jaxpr/cond
  337.4 25.7 %reshape.27 = bf16[64,192,383]{2,1,0:T(8,128)(2,1)} reshape(bf16[64,73536]{1,0:T(8,128)(2,1)} %slice.8) | data formatting | bytes 18825216 | tf_op jit(solution)/shard_map/while/body/eval_jaxpr/cond/branch_1_fun/reshape | solution.py:17
  370.2 59.7 %conditional.2 = (f32[192,1024]{0,1:T(8,128)S(1)}) conditional(s32[]{:T(128)} %convert_element_type.40, f32[192,1024]{0,1:T(8,128)S(1)} %get-tuple-element.193, (s32[]{:T(128)}, s32[]{:T(128)}, bf16[64,6144]{1,0:T(8,128)(2,1)S(1)}, bf16[16,192,1024]{1,2,0:T(8,128)(2,1)}, s32[]{:T(128)}, /*index=5*/f32[192,1024]{0,1:T(8,128)S(1)}) %tuple.36), branch_computations={%region_1.1_spmd, %region_2.2_spmd} | conditional | flops 75694088 | bytes 77020616 | solution.py:38
  398.3 25.7 %reshape.27 = bf16[64,192,383]{2,1,0:T(8,128)(2,1)} reshape(bf16[64,73536]{1,0:T(8,128)(2,1)} %slice.8) | data formatting | bytes 18825216 | tf_op jit(solution)/shard_map/while/body/eval_jaxpr/cond/branch_1_fun/reshape | solution.py:17
  431.1 59.7 %conditional.2 = (f32[192,1024]{0,1:T(8,128)S(1)}) conditional(s32[]{:T(128)} %convert_element_type.40, f32[192,1024]{0,1:T(8,128)S(1)} %get-tuple-element.193, (s32[]{:T(128)}, s32[]{:T(128)}, bf16[64,6144]{1,0:T(8,128)(2,1)S(1)}, bf16[16,192,1024]{1,2,0:T(8,128)(2,1)}, s32[]{:T(128)}, /*index=5*/f32[192,1024]{0,1:T(8,128)S(1)}) %tuple.36), branch_computations={%region_1.1_spmd, %region_2.2_spmd} | conditional | flops 75694088 | bytes 77020616 | solution.py:38
  436.1 13.3 %copy.17 = bf16[8,8,192,384]{3,1,2,0:T(8,128)(2,1)} copy(bf16[8,8,192,384]{3,2,1,0:T(8,128)(2,1)} %bitcast.18) | data formatting | bytes 18874368 | tf_op jit(solution)/shard_map/while/body/eval_jaxpr/cond
  459.2 25.7 %reshape.27 = bf16[64,192,383]{2,1,0:T(8,128)(2,1)} reshape(bf16[64,73536]{1,0:T(8,128)(2,1)} %slice.8) | data formatting | bytes 18825216 | tf_op jit(solution)/shard_map/while/body/eval_jaxpr/cond/branch_1_fun/reshape | solution.py:17
  492.0 59.7 %conditional.2 = (f32[192,1024]{0,1:T(8,128)S(1)}) conditional(s32[]{:T(128)} %convert_element_type.40, f32[192,1024]{0,1:T(8,128)S(1)} %get-tuple-element.193, (s32[]{:T(128)}, s32[]{:T(128)}, bf16[64,6144]{1,0:T(8,128)(2,1)S(1)}, bf16[16,192,1024]{1,2,0:T(8,128)(2,1)}, s32[]{:T(128)}, /*index=5*/f32[192,1024]{0,1:T(8,128)S(1)}) %tuple.36), branch_computations={%region_1.1_spmd, %region_2.2_spmd} | conditional | flops 75694088 | bytes 77020616 | solution.py:38
  497.0 13.3 %copy.17 = bf16[8,8,192,384]{3,1,2,0:T(8,128)(2,1)} copy(bf16[8,8,192,384]{3,2,1,0:T(8,128)(2,1)} %bitcast.18) | data formatting | bytes 18874368 | tf_op jit(solution)/shard_map/while/body/eval_jaxpr/cond
  520.2 25.7 %reshape.27 = bf16[64,192,383]{2,1,0:T(8,128)(2,1)} reshape(bf16[64,73536]{1,0:T(8,128)(2,1)} %slice.8) | data formatting | bytes 18825216 | tf_op jit(solution)/shard_map/while/body/eval_jaxpr/cond/branch_1_fun/reshape | solution.py:17
  552.9 59.7 %conditional.2 = (f32[192,1024]{0,1:T(8,128)S(1)}) conditional(s32[]{:T(128)} %convert_element_type.40, f32[192,1024]{0,1:T(8,128)S(1)} %get-tuple-element.193, (s32[]{:T(128)}, s32[]{:T(128)}, bf16[64,6144]{1,0:T(8,128)(2,1)S(1)}, bf16[16,192,1024]{1,2,0:T(8,128)(2,1)}, s32[]{:T(128)}, /*index=5*/f32[192,1024]{0,1:T(8,128)S(1)}) %tuple.36), branch_computations={%region_1.1_spmd, %region_2.2_spmd} | conditional | flops 75694088 | bytes 77020616 | solution.py:38
  557.9 13.3 %copy.17 = bf16[8,8,192,384]{3,1,2,0:T(8,128)(2,1)} copy(bf16[8,8,192,384]{3,2,1,0:T(8,128)(2,1)} %bitcast.18) | data formatting | bytes 18874368 | tf_op jit(solution)/shard_map/while/body/eval_jaxpr/cond
  581.1 25.7 %reshape.27 = bf16[64,192,383]{2,1,0:T(8,128)(2,1)} reshape(bf16[64,73536]{1,0:T(8,128)(2,1)} %slice.8) | data formatting | bytes 18825216 | tf_op jit(solution)/shard_map/while/body/eval_jaxpr/cond/branch_1_fun/reshape | solution.py:17
  613.9 59.7 %conditional.2 = (f32[192,1024]{0,1:T(8,128)S(1)}) conditional(s32[]{:T(128)} %convert_element_type.40, f32[192,1024]{0,1:T(8,128)S(1)} %get-tuple-element.193, (s32[]{:T(128)}, s32[]{:T(128)}, bf16[64,6144]{1,0:T(8,128)(2,1)S(1)}, bf16[16,192,1024]{1,2,0:T(8,128)(2,1)}, s32[]{:T(128)}, /*index=5*/f32[192,1024]{0,1:T(8,128)S(1)}) %tuple.36), branch_computations={%region_1.1_spmd, %region_2.2_spmd} | conditional | flops 75694088 | bytes 77020616 | solution.py:38
  642.0 25.7 %reshape.27 = bf16[64,192,383]{2,1,0:T(8,128)(2,1)} reshape(bf16[64,73536]{1,0:T(8,128)(2,1)} %slice.8) | data formatting | bytes 18825216 | tf_op jit(solution)/shard_map/while/body/eval_jaxpr/cond/branch_1_fun/reshape | solution.py:17
  674.8 59.7 %conditional.2 = (f32[192,1024]{0,1:T(8,128)S(1)}) conditional(s32[]{:T(128)} %convert_element_type.40, f32[192,1024]{0,1:T(8,128)S(1)} %get-tuple-element.193, (s32[]{:T(128)}, s32[]{:T(128)}, bf16[64,6144]{1,0:T(8,128)(2,1)S(1)}, bf16[16,192,1024]{1,2,0:T(8,128)(2,1)}, s32[]{:T(128)}, /*index=5*/f32[192,1024]{0,1:T(8,128)S(1)}) %tuple.36), branch_computations={%region_1.1_spmd, %region_2.2_spmd} | conditional | flops 75694088 | bytes 77020616 | solution.py:38
  679.8 13.3 %copy.17 = bf16[8,8,192,384]{3,1,2,0:T(8,128)(2,1)} copy(bf16[8,8,192,384]{3,2,1,0:T(8,128)(2,1)} %bitcast.18) | data formatting | bytes 18874368 | tf_op jit(solution)/shard_map/while/body/eval_jaxpr/cond
  702.9 25.7 %reshape.27 = bf16[64,192,383]{2,1,0:T(8,128)(2,1)} reshape(bf16[64,73536]{1,0:T(8,128)(2,1)} %slice.8) | data formatting | bytes 18825216 | tf_op jit(solution)/shard_map/while/body/eval_jaxpr/cond/branch_1_fun/reshape | solution.py:17
  735.7 59.7 %conditional.2 = (f32[192,1024]{0,1:T(8,128)S(1)}) conditional(s32[]{:T(128)} %convert_element_type.40, f32[192,1024]{0,1:T(8,128)S(1)} %get-tuple-element.193, (s32[]{:T(128)}, s32[]{:T(128)}, bf16[64,6144]{1,0:T(8,128)(2,1)S(1)}, bf16[16,192,1024]{1,2,0:T(8,128)(2,1)}, s32[]{:T(128)}, /*index=5*/f32[192,1024]{0,1:T(8,128)S(1)}) %tuple.36), branch_computations={%region_1.1_spmd, %region_2.2_spmd} | conditional | flops 75694088 | bytes 77020616 | solution.py:38
  740.7 13.3 %copy.17 = bf16[8,8,192,384]{3,1,2,0:T(8,128)(2,1)} copy(bf16[8,8,192,384]{3,2,1,0:T(8,128)(2,1)} %bitcast.18) | data formatting | bytes 18874368 | tf_op jit(solution)/shard_map/while/body/eval_jaxpr/cond
  763.9 25.7 %reshape.27 = bf16[64,192,383]{2,1,0:T(8,128)(2,1)} reshape(bf16[64,73536]{1,0:T(8,128)(2,1)} %slice.8) | data formatting | bytes 18825216 | tf_op jit(solution)/shard_map/while/body/eval_jaxpr/cond/branch_1_fun/reshape | solution.py:17
  796.7 59.7 %conditional.2 = (f32[192,1024]{0,1:T(8,128)S(1)}) conditional(s32[]{:T(128)} %convert_element_type.40, f32[192,1024]{0,1:T(8,128)S(1)} %get-tuple-element.193, (s32[]{:T(128)}, s32[]{:T(128)}, bf16[64,6144]{1,0:T(8,128)(2,1)S(1)}, bf16[16,192,1024]{1,2,0:T(8,128)(2,1)}, s32[]{:T(128)}, /*index=5*/f32[192,1024]{0,1:T(8,128)S(1)}) %tuple.36), branch_computations={%region_1.1_spmd, %region_2.2_spmd} | conditional | flops 75694088 | bytes 77020616 | solution.py:38
  801.6 13.3 %copy.17 = bf16[8,8,192,384]{3,1,2,0:T(8,128)(2,1)} copy(bf16[8,8,192,384]{3,2,1,0:T(8,128)(2,1)} %bitcast.18) | data formatting | bytes 18874368 | tf_op jit(solution)/shard_map/while/body/eval_jaxpr/cond
  824.8 25.7 %reshape.27 = bf16[64,192,383]{2,1,0:T(8,128)(2,1)} reshape(bf16[64,73536]{1,0:T(8,128)(2,1)} %slice.8) | data formatting | bytes 18825216 | tf_op jit(solution)/shard_map/while/body/eval_jaxpr/cond/branch_1_fun/reshape | solution.py:17
  857.6 59.7 %conditional.2 = (f32[192,1024]{0,1:T(8,128)S(1)}) conditional(s32[]{:T(128)} %convert_element_type.40, f32[192,1024]{0,1:T(8,128)S(1)} %get-tuple-element.193, (s32[]{:T(128)}, s32[]{:T(128)}, bf16[64,6144]{1,0:T(8,128)(2,1)S(1)}, bf16[16,192,1024]{1,2,0:T(8,128)(2,1)}, s32[]{:T(128)}, /*index=5*/f32[192,1024]{0,1:T(8,128)S(1)}) %tuple.36), branch_computations={%region_1.1_spmd, %region_2.2_spmd} | conditional | flops 75694088 | bytes 77020616 | solution.py:38
  885.7 25.7 %reshape.27 = bf16[64,192,383]{2,1,0:T(8,128)(2,1)} reshape(bf16[64,73536]{1,0:T(8,128)(2,1)} %slice.8) | data formatting | bytes 18825216 | tf_op jit(solution)/shard_map/while/body/eval_jaxpr/cond/branch_1_fun/reshape | solution.py:17
  918.5 59.7 %conditional.2 = (f32[192,1024]{0,1:T(8,128)S(1)}) conditional(s32[]{:T(128)} %convert_element_type.40, f32[192,1024]{0,1:T(8,128)S(1)} %get-tuple-element.193, (s32[]{:T(128)}, s32[]{:T(128)}, bf16[64,6144]{1,0:T(8,128)(2,1)S(1)}, bf16[16,192,1024]{1,2,0:T(8,128)(2,1)}, s32[]{:T(128)}, /*index=5*/f32[192,1024]{0,1:T(8,128)S(1)}) %tuple.36), branch_computations={%region_1.1_spmd, %region_2.2_spmd} | conditional | flops 75694088 | bytes 77020616 | solution.py:38
  923.5 13.3 %copy.17 = bf16[8,8,192,384]{3,1,2,0:T(8,128)(2,1)} copy(bf16[8,8,192,384]{3,2,1,0:T(8,128)(2,1)} %bitcast.18) | data formatting | bytes 18874368 | tf_op jit(solution)/shard_map/while/body/eval_jaxpr/cond
  946.7 25.7 %reshape.27 = bf16[64,192,383]{2,1,0:T(8,128)(2,1)} reshape(bf16[64,73536]{1,0:T(8,128)(2,1)} %slice.8) | data formatting | bytes 18825216 | tf_op jit(solution)/shard_map/while/body/eval_jaxpr/cond/branch_1_fun/reshape | solution.py:17
  979.4 59.7 %conditional.2 = (f32[192,1024]{0,1:T(8,128)S(1)}) conditional(s32[]{:T(128)} %convert_element_type.40, f32[192,1024]{0,1:T(8,128)S(1)} %get-tuple-element.193, (s32[]{:T(128)}, s32[]{:T(128)}, bf16[64,6144]{1,0:T(8,128)(2,1)S(1)}, bf16[16,192,1024]{1,2,0:T(8,128)(2,1)}, s32[]{:T(128)}, /*index=5*/f32[192,1024]{0,1:T(8,128)S(1)}) %tuple.36), branch_computations={%region_1.1_spmd, %region_2.2_spmd} | conditional | flops 75694088 | bytes 77020616 | solution.py:38
  984.4 13.3 %copy.17 = bf16[8,8,192,384]{3,1,2,0:T(8,128)(2,1)} copy(bf16[8,8,192,384]{3,2,1,0:T(8,128)(2,1)} %bitcast.18) | data formatting | bytes 18874368 | tf_op jit(solution)/shard_map/while/body/eval_jaxpr/cond
  1007.6 25.7 %reshape.27 = bf16[64,192,383]{2,1,0:T(8,128)(2,1)} reshape(bf16[64,73536]{1,0:T(8,128)(2,1)} %slice.8) | data formatting | bytes 18825216 | tf_op jit(solution)/shard_map/while/body/eval_jaxpr/cond/branch_1_fun/reshape | solution.py:17
  1040.3 28.8 %all_to_all.5 = bf16[8,192,1024]{2,1,0:T(8,128)(2,1)S(1)} all-to-all(bf16[8,192,1024]{2,1,0:T(8,128)(2,1)S(1)} %stack.2), channel_id=1, replica_groups=mesh['ctx'=16,'ch'=8] {'ch'}, dimensions={0} | all-to-all | bytes 6291456 | tf_op jit(solution)/shard_map/all_to_all | solution.py:49
  (183 shorter events, 398.2 us)
Async XLA Ops:
  6.5 46.6 %all-gather.2.cloned.1.call-start = ((), (), s32[]{:S(2)}) async-start(), calls=%async_computation.1 | async-start | bytes 6684672 | tf_op jit(solution)/shard_map/all_gather | solution.py:65
  64.2 975.4 %copy-start = (bf16[192,1024]{1,0:T(8,128)(2,1)S(1)}, bf16[192,1024]{1,0:T(8,128)(2,1)}, u32[]{:S(2)}) copy-start(bf16[192,1024]{1,0:T(8,128)(2,1)} %multiply_convert_fusion.1) | copy-start | bytes 1179652
  64.3 975.4 %copy-start.1 = (bf16[192,1024]{1,0:T(8,128)(2,1)S(1)}, bf16[192,1024]{1,0:T(8,128)(2,1)}, u32[]{:S(2)}) copy-start(bf16[192,1024]{1,0:T(8,128)(2,1)} %param.10) | copy-start | bytes 1179652
  64.3 975.4 %copy-start.2 = (f32[1024]{0:T(1024)S(1)}, f32[1024]{0:T(1024)}, u32[]{:S(2)}) copy-start(f32[1024]{0:T(1024)} %param.14) | copy-start | bytes 12292
  1039.7 29.8 %copy-start.3 = (bf16[8192,1024]{1,0:T(8,128)(2,1)S(1)}, bf16[8192,1024]{1,0:T(8,128)(2,1)}, u32[]{:S(2)}) copy-start(bf16[8192,1024]{1,0:T(8,128)(2,1)} %param.15) | copy-start | bytes 50331652
Sparse Core Ops, SparseCore 0:
  9.0 44.0 all-gather.1
